TPU v7x, 32 devices: a whole 2x2x4 slice. The times are simulated.
32 devices in a mesh: groups: 2 (over x), frames: 16 (over z, y, core).
Axes of the slice: x: 2, y: 2, z: 4, core: 2. Of those that a mesh axis runs over, the one named last changes fastest.
Arguments:
- video: bfloat16 [4, 16, 128, 1024], P('groups', 'frames'), parts along dimension 0, may hold values from -70 to 70
- w_qkv: bfloat16 [1024, 3072], replicated, may hold values from -8 to 8
- w_out: bfloat16 [1024, 1024], replicated, may hold values from -0.1875 to 0.1875
- keep_list: int32 [4, 16, 128], P('groups', 'frames'), parts along dimension 0, may hold values from 0 to 127, each once within a row
- kept_counts: int32 [4, 16], P('groups', 'frames'), parts along dimension 0, may hold values from 1 to 4, 32 in all within a row
- w_proj: bfloat16 [1024, 8192], P(None, 'frames'), may hold values from -20 to 20
- llm_gain: bfloat16 [8192], P('frames'), may hold values from 0.099609375 to 1.8984375
- w_gate: bfloat16 [8192, 16384], P(None, 'frames'), may hold values from -0.0625 to 0.0625
- w_up: bfloat16 [8192, 16384], P(None, 'frames'), may hold values from -0.0625 to 0.0625
Outputs:
- llm_hidden: bfloat16 [4, 32, 16384], P('groups', None, 'frames'), parts along dimension 0
There are 2 independent parts, one for each index of `groups`. A program takes and returns all parts, laid end to end along the dimension named above; an argument that names none is the same for every part. Nothing has to cross between parts.
Inputs may be any that keep to these rules, and one draw needn't show every extreme that they name: `keep_list`: each row of a frame lists every patch index once. `kept_counts`: the counts of one video sum to 32.
All inputs are finite; a program needn't handle non-finite values. No bound on the sum of `kept_counts` on one device may be relied on, other than what follows from the above.
Results may differ from a plain program's by a relative error of at most 0.0076.
Values may be sent and summed in bfloat16 or wider, within the bound.
No kernel may reach another device: no remote copies, remote signals or barrier semaphores. Data moves between devices by JAX's collectives and lax.ppermute only.
A program may use at most 128 MiB of HBM per device.

v0:
```python
import jax
import jax.numpy as jnp
from jax import lax
from jax.sharding import PartitionSpec as P

HEAD_DIM = 64
DL = 8192
TOKL = 2
KMAX = 4
NORM_EPS = 1e-05
SCORE_SCALE = 0.125


def layer_norm(values):
    floated = values.astype(jnp.float32)
    average = jnp.mean(floated, axis=-1, keepdims=True)
    centred = floated - average
    variance = jnp.mean(centred * centred, axis=-1, keepdims=True)
    return (centred * lax.rsqrt(variance + NORM_EPS)).astype(jnp.bfloat16)


def sequence_slots(counts, seq_len, slot_width):
    offsets = jnp.cumsum(counts, axis=1) - counts
    positions = lax.broadcasted_iota(jnp.int32, (counts.shape[0], seq_len), 1)
    started = (offsets[:, None, :] <= positions[:, :, None]).astype(jnp.int32)
    owner_frame = jnp.sum(started, axis=2) - 1
    frame_ids = lax.broadcasted_iota(jnp.int32, started.shape, 2)
    begin_at = jnp.sum(
        jnp.where(frame_ids == owner_frame[:, :, None], offsets[:, None, :], 0), axis=2
    )
    return owner_frame * slot_width + positions - begin_at


def temporal_attention(queries, keys_in, values_in):
    scores = (
        jnp.einsum("vfphe,vgphe->vphfg", queries, keys_in, preferred_element_type=jnp.float32)
        * SCORE_SCALE
    )
    largest = jnp.max(scores, axis=-1, keepdims=True)
    weights_exp = jnp.exp(scores - largest)
    weights = (weights_exp / jnp.sum(weights_exp, axis=-1, keepdims=True)).astype(jnp.bfloat16)
    return jnp.einsum(
        "vphfg,vgphe->vfphe", weights, values_in, preferred_element_type=jnp.float32
    ).astype(jnp.bfloat16)


def take_frame_rows(frame_rows, picks_row):
    return jnp.take(frame_rows, picks_row, axis=0)


def local(video, w_qkv, w_out, keep_list, kept_counts, w_proj, llm_gain, w_gate, w_up):
    videos = video.shape[0]
    patches = video.shape[2]
    model_width = video.shape[3]
    devices = lax.axis_size("frames")
    head_count = model_width // HEAD_DIM
    all_counts = lax.all_gather(kept_counts, "frames", axis=1, tiled=True)
    normed = layer_norm(video)

    def split_heads(tensor_in):
        return tensor_in.reshape(tensor_in.shape[:3] + (head_count, HEAD_DIM))

    received = lax.all_to_all(normed, "frames", split_axis=2, concat_axis=1, tiled=True)
    projected_here = jnp.dot(
        received.reshape(-1, model_width), w_qkv, preferred_element_type=jnp.float32
    ).astype(jnp.bfloat16)
    projected_here = projected_here.reshape(received.shape[:3] + (3 * model_width,))
    queries = split_heads(projected_here[..., :model_width])
    keys_in = split_heads(projected_here[..., model_width : 2 * model_width])
    values_in = split_heads(projected_here[..., 2 * model_width :])
    attended = temporal_attention(queries, keys_in, values_in)
    attended = attended.reshape(projected_here.shape[:3] + (model_width,))
    returned = lax.all_to_all(attended, "frames", split_axis=1, concat_axis=2, tiled=True)
    encoded = (
        video.astype(jnp.float32).reshape(-1, model_width)
        + jnp.dot(returned.reshape(-1, model_width), w_out, preferred_element_type=jnp.float32)
    ).astype(jnp.bfloat16)
    encoded = encoded.reshape(videos, patches, model_width)
    chosen = keep_list[:, 0, :KMAX]
    picked = jax.vmap(take_frame_rows)(encoded, chosen)
    slot_index = lax.broadcasted_iota(jnp.int32, (videos, KMAX), 1)
    live_slots = slot_index < kept_counts
    slot_rows = jnp.where(live_slots[:, :, None], picked, jnp.zeros_like(picked))
    gathered_slots = lax.all_gather(slot_rows, "frames", axis=1, tiled=True)
    sequence_order = sequence_slots(all_counts, devices * TOKL, KMAX)
    local_cols = jnp.dot(
        gathered_slots.reshape(-1, model_width), w_proj, preferred_element_type=jnp.float32
    )
    local_cols = local_cols.reshape(gathered_slots.shape[0], gathered_slots.shape[1], -1)
    squares = lax.psum(jnp.sum(local_cols * local_cols, axis=2), "frames")
    row_scale = lax.rsqrt(squares / DL + NORM_EPS)
    normed_cols = (local_cols * row_scale[:, :, None] * llm_gain.astype(jnp.float32)).astype(
        jnp.bfloat16
    )
    hidden_width = w_gate.shape[1]
    zero_sums = jnp.zeros(
        (gathered_slots.shape[0], gathered_slots.shape[1], hidden_width), jnp.float32
    )
    column_piece = lax.all_gather(normed_cols, "frames", axis=2, tiled=True)
    piece_width = column_piece.shape[2]
    flat_piece = column_piece.reshape(-1, piece_width)
    gate_more = jnp.dot(flat_piece, w_gate, preferred_element_type=jnp.float32).reshape(
        zero_sums.shape
    )
    up_more = jnp.dot(flat_piece, w_up, preferred_element_type=jnp.float32).reshape(zero_sums.shape)
    hidden_slots = (jax.nn.silu(gate_more) * up_more).astype(jnp.bfloat16)
    llm_hidden = jax.vmap(take_frame_rows)(hidden_slots, sequence_order)
    return llm_hidden


def solution(mesh):
    in_specs = (
        P("groups", "frames", None, None),
        P(),
        P(),
        P("groups", "frames", None),
        P("groups", "frames"),
        P(None, "frames"),
        P("frames"),
        P(None, "frames"),
        P(None, "frames"),
    )
    out_specs = P("groups", None, "frames")
    return jax.shard_map(local, mesh=mesh, in_specs=in_specs, out_specs=out_specs, check_vma=False)
```

profile of v0, /device:TPU:0, one launch (start us, length us, event | category | flops | bytes accessed | tf_op | source)
XLA Modules:
  0.0 195.9 jit_solution(10785479989955932589)
XLA Ops:
  6.5 0.0 copy-start
  6.5 1.7 convert_reduce_fusion
  8.3 1.9 multiply_reduce_fusion.1
  10.2 1.7 multiply_convert_fusion
  12.0 21.5 %all_to_all.8 = bf16[2,1,128,1024]{3,0,1,2:T(2,128)(2,1)S(1)} all-to-all(bf16[2,1,128,1024]{3,0,1,2:T(2,128)(2,1)S(1)} %multiply_convert_fusion), channel_id=1, replica_groups=mesh['groups'=2,'frames'=16] {'frames'}, dimensions={2} | all-to-all | bytes 1048576 | tf_op jit(solution)/shard_map/all_to_all | solution.py:63
  33.5 0.1 copy.62
  33.6 4.6 %convolution_convert_fusion = bf16[256,3072]{1,0:T(8,128)(2,1)S(1)} fusion(bf16[256,1024]{1,0:T(8,128)(2,1)S(1)} %bitcast.65, bf16[1024,3072]{1,0:T(8,128)(2,1)} %param.10), kind=kOutput, calls=%fused_computation.7 | convolution fusion | flops 1611399168 | bytes 8388608 | tf_op jit(solution)/shard_map/dot_general | solution.py:64
  38.2 0.9 fusion.42
  39.1 2.5 %reshape.177 = bf16[2,16,8,16,64]{4,3,2,1,0:T(8,128)(2,1)} reshape(bf16[2,16,8,1024]{3,2,1,0:T(8,128)(2,1)} %get-tuple-element.7) | data formatting | bytes 1048576 | tf_op jit(solution)/shard_map/reshape | solution.py:61
  41.6 1.6 reshape.178
  43.2 1.6 reshape.176
  44.9 0.0 copy-start.3
  44.9 4.9 %fusion.43 = (f32[2,8,16,16]{3,2,1,0:T(8,128)S(1)}, f32[2,8,16,16,16]{3,4,2,1,0:T(8,128)}) fusion(bf16[2,16,8,16,64]{4,3,2,1,0:T(8,128)(2,1)} %reshape.178, bf16[2,16,8,16,64]{4,3,2,1,0:T(8,128)(2,1)} %reshape.177), kind=kOutput, calls=%fused_computation.62 | convolution fusion | flops 8585231 | bytes 1327104 | tf_op jit(solution)/shard_map/sub | solution.py:40
  49.8 0.0 copy-done.3
  49.8 2.5 %fusion.6 = bf16[2,16,8,16,64]{4,1,3,2,0:T(8,128)(2,1)S(1)} fusion(f32[2,8,16,16,16]{3,4,2,1,0:T(8,128)} %get-tuple-element.9, bf16[2,16,8,16,64]{4,3,2,1,0:T(8,128)(2,1)S(1)} %copy-done.3, f32[2,8,16,16]{3,2,1,0:T(8,128)S(1)} %get-tuple-element.8), kind=kOutput, calls=%fused_computation.13 | convolution fusion | flops 8781824 | bytes 1327104 | tf_op jit(solution)/shard_map/vphfg,vgphe->vfphe/dot_general | solution.py:42
  52.2 0.0 copy-start.2
  52.3 1.3 copy.73
  53.5 2.6 %reshape.201 = bf16[2,16,8,1024]{3,2,0,1:T(8,128)(2,1)} reshape(bf16[2,16,8,16,64]{4,3,2,0,1:T(8,128)(2,1)} %copy.73) | data formatting | bytes 1048576 | tf_op jit(solution)/shard_map/reshape | solution.py:72
  56.1 4.2 %all-to-all-start.1 = ((bf16[2,16,8,1024]{3,2,0,1:T(8,128)(2,1)}), bf16[2,16,8,1024]{3,2,0,1:T(8,128)(2,1)}, u32[]{:S(2)}, u32[]{:S(2)}) async-start(bf16[2,16,8,1024]{3,2,0,1:T(8,128)(2,1)} %reshape.201), calls=%async_computation.1 | async-start | bytes 1048576 | tf_op jit(solution)/shard_map/all_to_all | solution.py:73
  60.4 0.0 copy-start.5
  60.4 0.0 copy-start.4
  60.4 0.0 copy-start.6
  60.4 0.2 all-gather.3.cloned.1.call-start
  60.6 0.0 copy-done.2
  60.6 0.5 copy_convert_fusion
  61.2 0.3 copy.61
  61.5 0.0 copy-done.5
  61.6 0.1 reshape.182
  61.7 0.1 copy.59
  61.8 0.0 copy-done.4
  61.8 0.0 copy-done.6
  61.8 12.9 %all-to-all-done.1 = bf16[2,16,8,1024]{3,2,0,1:T(8,128)(2,1)} async-done(((bf16[2,16,8,1024]{3,2,0,1:T(8,128)(2,1)}), bf16[2,16,8,1024]{3,2,0,1:T(8,128)(2,1)}, u32[]{:S(2)}, u32[]{:S(2)}) %all-to-all-start.1) | async-done | bytes 524320 | tf_op jit(solution)/shard_map/all_to_all | solution.py:73
  74.7 1.1 copy.69
  75.7 0.0 copy-done
  75.8 1.5 fusion.7
  77.3 1.3 gather_fusion
  78.6 0.1 broadcast_select_fusion.2
  78.7 20.6 %all_gather.10 = bf16[2,64,1024]{2,0,1:T(2,128)(2,1)S(1)} all-gather(bf16[2,4,1024]{2,0,1:T(2,128)(2,1)S(1)} %broadcast_select_fusion.2), channel_id=1, replica_groups=mesh['groups'=2,'frames'=16] {'frames'}, dimensions={1}, use_global_device_ids=true | all-gather | bytes 278528 | tf_op jit(solution)/shard_map/all_gather | solution.py:84
  99.3 1.6 multiply_reduce_fusion.2
  100.9 29.8 %psum.7 = f32[2,64]{1,0:T(2,128)S(1)} all-reduce(f32[2,64]{1,0:T(2,128)S(1)} %get-tuple-element.10), channel_id=1, replica_groups=mesh['groups'=2,'frames'=16] {'frames'}, use_global_device_ids=true, to_apply=%region_8.9 | all-reduce | flops 128 | bytes 1024 | tf_op jit(solution)/shard_map/psum | solution.py:90
  130.7 0.8 multiply_convert_fusion.1
  131.5 0.0 all-gather.3.cloned.1.call-update
  131.5 17.1 %all-gather = s32[16,1,2]{2,1,0:T(1,128)S(1)} all-gather(s32[1,1,2]{2,1,0:T(1,128)S(1)} %bitcast.70), channel_id=1, replica_groups=mesh['groups'=2,'frames'=16] {'frames'}, dimensions={0}, use_global_device_ids=true | all-gather | bytes 136 | tf_op jit(solution)/shard_map/all_gather | solution.py:57
  148.7 0.1 copy.58
  148.7 0.2 reduce_window_sum.11
  148.9 0.1 convert_reduce_fusion.1
  149.0 0.1 select_reduce_fusion
  149.1 0.1 reshape.188
  149.2 20.7 %all-gather.3.cloned.1.call-done = bf16[2,64,8192]{2,1,0:T(8,128)(2,1)} async-done(((bf16[2,64,512]{2,1,0:T(8,128)(2,1)}), bf16[2,64,8192]{2,1,0:T(8,128)(2,1)}) %all-gather.3.cloned.1.call-update) | async-done | bytes 2097168 | tf_op jit(solution)/shard_map/all_gather | solution.py:99
  169.9 0.0 copy-start.1
  169.9 8.9 %fusion.3 = f32[2,64,1024]{2,1,0:T(8,128)S(1)} fusion(bf16[2,64,8192]{2,1,0:T(8,128)(2,1)} %all-gather.3.cloned.1.call-done, bf16[8192,1024]{1,0:T(8,128)(2,1)} %param.16), kind=kOutput, calls=%fused_computation.5 | convolution fusion | flops 2147483648 | bytes 19398656 | tf_op jit(solution)/shard_map/dot_general | solution.py:102
  178.8 0.0 copy-done.1
  178.8 8.3 %fusion.11 = bf16[2,64,1024]{2,1,0:T(8,128)(2,1)S(1)} fusion(bf16[2,64,8192]{2,1,0:T(8,128)(2,1)S(1)} %copy-done.1, bf16[8192,1024]{1,0:T(8,128)(2,1)} %param.17, f32[2,64,1024]{2,1,0:T(8,128)S(1)} %fusion.3), kind=kOutput, calls=%fused_computation.17 | convolution fusion | flops 2148270080 | bytes 19660800 | tf_op jit(solution)/shard_map/dot_general | solution.py:105
  187.2 1.1 gather_fusion.1
  188.3 0.7 broadcast_select_fusion
  (12 shorter events, 0.1 us)
Async XLA Ops:
  6.5 69.2 %copy-start = (bf16[1024,1024]{1,0:T(8,128)(2,1)S(1)}, bf16[1024,1024]{1,0:T(8,128)(2,1)}, u32[]{:S(2)}) copy-start(bf16[1024,1024]{1,0:T(8,128)(2,1)} %param.11) | copy-start | bytes 6291460
  44.9 4.9 %copy-start.3 = (bf16[2,16,8,16,64]{4,3,2,1,0:T(8,128)(2,1)S(1)}, bf16[2,16,8,16,64]{4,3,2,1,0:T(8,128)(2,1)}, u32[]{:S(2)}) copy-start(bf16[2,16,8,16,64]{4,3,2,1,0:T(8,128)(2,1)} %reshape.176) | copy-start | bytes 1572868
  52.2 8.4 %copy-start.2 = (bf16[2,1,128,1024]{3,2,1,0:T(8,128)(2,1)S(1)}, bf16[2,1,128,1024]{3,2,1,0:T(8,128)(2,1)}, u32[]{:S(2)}) copy-start(bf16[2,1,128,1024]{3,2,1,0:T(8,128)(2,1)} %param.9) | copy-start | bytes 1572868
  56.1 18.5 %all-to-all-start.1 = ((bf16[2,16,8,1024]{3,2,0,1:T(8,128)(2,1)}), bf16[2,16,8,1024]{3,2,0,1:T(8,128)(2,1)}, u32[]{:S(2)}, u32[]{:S(2)}) async-start(bf16[2,16,8,1024]{3,2,0,1:T(8,128)(2,1)} %reshape.201), calls=%async_computation.1 | async-start | bytes 1048576 | tf_op jit(solution)/shard_map/all_to_all | solution.py:73
  60.4 1.2 copy-start.5
  60.4 1.4 copy-start.4
  60.4 1.4 copy-start.6
  60.4 109.5 %all-gather.3.cloned.1.call-start = ((), (), s32[]{:S(2)}) async-start(), calls=%async_computation.2 | async-start | bytes 2228224 | tf_op jit(solution)/shard_map/all_gather | solution.py:99
  169.9 8.9 %copy-start.1 = (bf16[2,64,8192]{2,1,0:T(8,128)(2,1)S(1)}, bf16[2,64,8192]{2,1,0:T(8,128)(2,1)}, u32[]{:S(2)}) copy-start(bf16[2,64,8192]{2,1,0:T(8,128)(2,1)} %all-gather.3.cloned.1.call-done) | copy-start | bytes 6291460
Sparse Core Ops, SparseCore 0:
  131.6 38.2 all-gather.2
where the time goes:
time: 197 us; the launch traced here: 196 us
  blocking collectives  89.1 us (45%)
  waiting for transfers between devices  33.6 us (17%)
  matrix products  32.3 us (16%)
  local copies, waits for them, and re-layouts  14.9 us (8%)
  between operations  13.6 us (7%)
  other arithmetic  7.99 us (4%)
  starting transfers between devices  4.46 us (2%)
    psum x1, blocking collectives, local(): squares = lax.psum(jnp.sum(local_cols * local_cols, axis=2), 'frames')  29.8 us
    all_to_all x1, blocking collectives, local(): lax.all_to_all(normed, 'frames', split_axis=2, concat_axis=1, tiled=True)  21.5 us
    all_gather x1, waiting for transfers between devices, local(): column_piece = lax.all_gather(normed_cols, 'frames', axis=2, tiled=True)  20.7 us
    all_gather x1, blocking collectives, local(): gathered_slots = lax.all_gather(slot_rows, 'frames', axis=1, tiled=True)  20.6 us
    all_gather x1, blocking collectives, local(): all_counts = lax.all_gather(kept_counts, 'frames', axis=1, tiled=True)  17.1 us
    all_to_all x1, waiting for transfers between devices, local(): lax.all_to_all(attended, 'frames', split_axis=1, concat_axis=2, tiled=True)  12.9 us
    dot_general x1, matrix products, local(): jnp.dot(flat_piece, w_gate, preferred_element_type=jnp.float32)  8.87 us
    dot_general x1, matrix products, local(): jnp.dot(flat_piece, w_up, preferred_element_type=jnp.float32)  8.34 us
  transfers between devices with their start and end apart: 2, of which 2 were waited for; matrix products, arithmetic and copies ran while one was open for 1% of the time, Pallas kernels for 0%

commit v1 on v0

--- a/solution.py
+++ b/solution.py
@@ -81,7 +81,18 @@
     slot_index = lax.broadcasted_iota(jnp.int32, (videos, KMAX), 1)
     live_slots = slot_index < kept_counts
     slot_rows = jnp.where(live_slots[:, :, None], picked, jnp.zeros_like(picked))
-    gathered_slots = lax.all_gather(slot_rows, "frames", axis=1, tiled=True)
+    base_arr = jax.lax.psum(1, axis_name="frames")
+    prior = jax.lax.axis_index("frames")
+    response, z = (base_arr, prior)
+    gathered_slots, low = (slot_rows, 1)
+    while low < response:
+        y_new = jax.lax.ppermute(
+            gathered_slots, "frames", tuple(((rr, rr ^ low) for rr in range(response)))
+        )
+        kept_arr = jnp.concatenate([gathered_slots, y_new], 1)
+        passed = jnp.concatenate([y_new, gathered_slots], axis=1)
+        gathered_slots = jnp.where(z & low == 0, kept_arr, passed)
+        low = 2 * low
     sequence_order = sequence_slots(all_counts, devices * TOKL, KMAX)
     local_cols = jnp.dot(
         gathered_slots.reshape(-1, model_width), w_proj, preferred_element_type=jnp.float32

time: 197 us -> 193 us (0.980)
  blocking collectives: 89.1 us -> 68.1 us
  waiting for transfers between devices: 33.6 us -> 45.1 us
  starting transfers between devices: 4.46 us -> 9.94 us
    all_gather x1 -> x0, blocking collectives: 20.6 us -> none  [local(): gathered_slots = lax.all_gather(slot_rows, 'frames', axis=1, tiled=True)]
    ppermute x0 -> x4, waiting for transfers between devices: none -> 11.4 us  [local(): jax.lax.ppermute(gathered_slots, 'frames', tuple(((rr, rr ^ low) for rr i...]
    ppermute x0 -> x4, starting transfers between devices: none -> 5.48 us  [local(): jax.lax.ppermute(gathered_slots, 'frames', tuple(((rr, rr ^ low) for rr i...]
  transfers between devices with their start and end apart: 2 -> 6, of which waited for: 2 -> 6; matrix products, arithmetic and copies ran while one was open for 1% -> 1% of each run, Pallas kernels for 0% -> 0%
where the time goes in v1:
time: 193 us; the launch traced here: 192 us
  blocking collectives  68.1 us (35%)
  waiting for transfers between devices  45.1 us (23%)
  matrix products  32.3 us (17%)
  local copies, waits for them, and re-layouts  14.8 us (8%)
  between operations  13.6 us (7%)
  starting transfers between devices  9.94 us (5%)
  other arithmetic  8.12 us (4%)
    psum x1, blocking collectives, local(): squares = lax.psum(jnp.sum(local_cols * local_cols, axis=2), 'frames')  29.5 us
    all_to_all x1, blocking collectives, local(): lax.all_to_all(normed, 'frames', split_axis=2, concat_axis=1, tiled=True)  21.5 us
    all_gather x1, waiting for transfers between devices, local(): column_piece = lax.all_gather(normed_cols, 'frames', axis=2, tiled=True)  20.8 us
    all_gather x1, blocking collectives, local(): all_counts = lax.all_gather(kept_counts, 'frames', axis=1, tiled=True)  17.2 us
    all_to_all x1, waiting for transfers between devices, local(): lax.all_to_all(attended, 'frames', split_axis=1, concat_axis=2, tiled=True)  13 us
    ppermute x4, waiting for transfers between devices, local(): jax.lax.ppermute(gathered_slots, 'frames', tuple(((rr, rr ^ low) for rr i...  11.4 us
    dot_general x1, matrix products, local(): jnp.dot(flat_piece, w_gate, preferred_element_type=jnp.float32)  8.87 us
    dot_general x1, matrix products, local(): jnp.dot(flat_piece, w_up, preferred_element_type=jnp.float32)  8.34 us
  transfers between devices with their start and end apart: 6, of which 6 were waited for; matrix products, arithmetic and copies ran while one was open for 1% of the time, Pallas kernels for 0%

profile of v1, /device:TPU:0, one launch (start us, length us, event | category | flops | bytes accessed | tf_op | source)
XLA Modules:
  0.0 192.0 jit_solution(10095998272529131313)
XLA Ops:
  6.5 0.0 copy-start
  6.5 1.7 convert_reduce_fusion
  8.3 1.9 %multiply_reduce_fusion.1 = f32[2,128]{0,1:T(8,128)S(1)} fusion(f32[2,128]{0,1:T(8,128)S(1)} %broadcast_multiply_fusion, bf16[2,1,128,1024]{3,2,1,0:T(8,128)(2,1)} %param.9), kind=kLoop, calls=%fused_computation.27 | loop fusion | flops 1048320 | bytes 526336 | tf_op jit(solution)/shard_map/reduce_sum | solution.py:18
  10.2 1.7 multiply_convert_fusion
  12.0 21.5 %all_to_all.8 = bf16[2,1,128,1024]{3,0,1,2:T(2,128)(2,1)S(1)} all-to-all(bf16[2,1,128,1024]{3,0,1,2:T(2,128)(2,1)S(1)} %multiply_convert_fusion), channel_id=1, replica_groups=mesh['groups'=2,'frames'=16] {'frames'}, dimensions={2} | all-to-all | bytes 1048576 | tf_op jit(solution)/shard_map/all_to_all | solution.py:63
  33.5 0.1 copy.52
  33.6 4.6 %convolution_convert_fusion = bf16[256,3072]{1,0:T(8,128)(2,1)S(1)} fusion(bf16[256,1024]{1,0:T(8,128)(2,1)S(1)} %bitcast.65, bf16[1024,3072]{1,0:T(8,128)(2,1)} %param.10), kind=kOutput, calls=%fused_computation.7 | convolution fusion | flops 1611399168 | bytes 8388608 | tf_op jit(solution)/shard_map/dot_general | solution.py:64
  38.2 0.9 fusion.48
  39.1 2.5 %reshape.178 = bf16[2,16,8,16,64]{4,3,2,1,0:T(8,128)(2,1)} reshape(bf16[2,16,8,1024]{3,2,1,0:T(8,128)(2,1)} %get-tuple-element.7) | data formatting | bytes 1048576 | tf_op jit(solution)/shard_map/reshape | solution.py:61
  41.6 1.6 reshape.179
  43.2 1.6 reshape.177
  44.9 0.0 copy-start.3
  44.9 4.9 %fusion.49 = (f32[2,8,16,16]{3,2,1,0:T(8,128)S(1)}, f32[2,8,16,16,16]{3,4,2,1,0:T(8,128)}) fusion(bf16[2,16,8,16,64]{4,3,2,1,0:T(8,128)(2,1)} %reshape.179, bf16[2,16,8,16,64]{4,3,2,1,0:T(8,128)(2,1)} %reshape.178), kind=kOutput, calls=%fused_computation.71 | convolution fusion | flops 8585231 | bytes 1327104 | tf_op jit(solution)/shard_map/sub | solution.py:40
  49.8 0.0 copy-done.3
  49.8 2.5 %fusion.6 = bf16[2,16,8,16,64]{4,1,3,2,0:T(8,128)(2,1)S(1)} fusion(f32[2,8,16,16,16]{3,4,2,1,0:T(8,128)} %get-tuple-element.9, bf16[2,16,8,16,64]{4,3,2,1,0:T(8,128)(2,1)S(1)} %copy-done.3, f32[2,8,16,16]{3,2,1,0:T(8,128)S(1)} %get-tuple-element.8), kind=kOutput, calls=%fused_computation.13 | convolution fusion | flops 8781824 | bytes 1327104 | tf_op jit(solution)/shard_map/vphfg,vgphe->vfphe/dot_general | solution.py:42
  52.2 0.0 copy-start.2
  52.3 1.3 copy.61
  53.5 2.6 %reshape.202 = bf16[2,16,8,1024]{3,2,0,1:T(8,128)(2,1)} reshape(bf16[2,16,8,16,64]{4,3,2,0,1:T(8,128)(2,1)} %copy.61) | data formatting | bytes 1048576 | tf_op jit(solution)/shard_map/reshape | solution.py:72
  56.1 4.2 %all-to-all-start.1 = ((bf16[2,16,8,1024]{3,2,0,1:T(8,128)(2,1)}), bf16[2,16,8,1024]{3,2,0,1:T(8,128)(2,1)}, u32[]{:S(2)}, u32[]{:S(2)}) async-start(bf16[2,16,8,1024]{3,2,0,1:T(8,128)(2,1)} %reshape.202), calls=%async_computation.1 | async-start | bytes 1048576 | tf_op jit(solution)/shard_map/all_to_all | solution.py:73
  60.4 0.0 copy-start.5
  60.4 0.0 copy-start.6
  60.4 0.2 all-gather.3.cloned.1.call-start
  60.6 0.0 copy-done.2
  60.6 0.5 copy_convert_fusion
  61.2 0.3 copy.51
  61.5 0.0 copy-done.5
  61.5 0.1 reshape.183
  61.6 0.0 copy-done.6
  61.6 0.1 iota_compare_fusion.2
  61.7 13.0 %all-to-all-done.1 = bf16[2,16,8,1024]{3,2,0,1:T(8,128)(2,1)} async-done(((bf16[2,16,8,1024]{3,2,0,1:T(8,128)(2,1)}), bf16[2,16,8,1024]{3,2,0,1:T(8,128)(2,1)}, u32[]{:S(2)}, u32[]{:S(2)}) %all-to-all-start.1) | async-done | bytes 524320 | tf_op jit(solution)/shard_map/all_to_all | solution.py:73
  74.7 1.1 copy.59
  75.7 0.0 copy-done
  75.8 0.0 copy-start.4
  75.8 1.5 fusion.7
  77.3 1.3 gather_fusion
  78.6 0.1 select_select_fusion
  78.7 0.2 collective-permute-start
  78.9 1.0 collective-permute-done
  80.0 1.1 collective-permute-start.1
  81.1 2.8 %collective-permute-done.1 = bf16[2,8,1024]{2,1,0:T(8,128)(2,1)S(1)} collective-permute-done((bf16[2,8,1024]{2,1,0:T(8,128)(2,1)S(1)}, bf16[2,8,1024]{2,1,0:T(8,128)(2,1)S(1)}, u32[]{:S(2)}, u32[]{:S(2)}) %collective-permute-start.1) | collective-permute-done | bytes 32800 | tf_op jit(solution)/shard_map/ppermute | solution.py:89
  84.0 1.6 collective-permute-start.2
  85.6 2.7 %collective-permute-done.2 = bf16[2,16,1024]{2,1,0:T(8,128)(2,1)S(1)} collective-permute-done((bf16[2,16,1024]{2,1,0:T(8,128)(2,1)S(1)}, bf16[2,16,1024]{2,1,0:T(8,128)(2,1)S(1)}, u32[]{:S(2)}, u32[]{:S(2)}) %collective-permute-start.2) | collective-permute-done | bytes 65568 | tf_op jit(solution)/shard_map/ppermute | solution.py:89
  88.3 2.5 %collective-permute-start.3 = (bf16[2,32,1024]{2,1,0:T(8,128)(2,1)S(1)}, bf16[2,32,1024]{2,1,0:T(8,128)(2,1)S(1)}, u32[]{:S(2)}, u32[]{:S(2)}) collective-permute-start(bf16[2,32,1024]{2,1,0:T(8,128)(2,1)S(1)} %maximum_select_fusion.2), channel_id=1, source_target_pairs={{0,8},{1,9},{2,10},{3,11},{4,12},{5,13},{6,14},{7,15},{8,0},{9,1},... | collective-permute-start | bytes 393224 | tf_op jit(solution)/shard_map/ppermute | solution.py:89
  90.8 0.0 copy-done.4
  90.8 4.8 %collective-permute-done.3 = bf16[2,32,1024]{2,1,0:T(8,128)(2,1)S(1)} collective-permute-done((bf16[2,32,1024]{2,1,0:T(8,128)(2,1)S(1)}, bf16[2,32,1024]{2,1,0:T(8,128)(2,1)S(1)}, u32[]{:S(2)}, u32[]{:S(2)}) %collective-permute-start.3) | collective-permute-done | bytes 131104 | tf_op jit(solution)/shard_map/ppermute | solution.py:89
  95.7 1.6 multiply_reduce_fusion.2
  97.3 29.5 %psum.7 = f32[2,64]{1,0:T(2,128)S(1)} all-reduce(f32[2,64]{1,0:T(2,128)S(1)} %get-tuple-element.10), channel_id=1, replica_groups=mesh['groups'=2,'frames'=16] {'frames'}, use_global_device_ids=true, to_apply=%region_8.9 | all-reduce | flops 128 | bytes 1024 | tf_op jit(solution)/shard_map/psum | solution.py:101
  126.8 0.8 multiply_convert_fusion.1
  127.5 0.0 all-gather.3.cloned.1.call-update
  127.6 17.2 %all-gather = s32[16,1,2]{2,1,0:T(1,128)S(1)} all-gather(s32[1,1,2]{2,1,0:T(1,128)S(1)} %bitcast.70), channel_id=1, replica_groups=mesh['groups'=2,'frames'=16] {'frames'}, dimensions={0}, use_global_device_ids=true | all-gather | bytes 136 | tf_op jit(solution)/shard_map/all_gather | solution.py:57
  144.7 0.1 copy.49
  144.8 0.2 reduce_window_sum.11
  145.0 0.1 convert_reduce_fusion.1
  145.1 0.1 select_reduce_fusion
  145.2 0.1 reshape.189
  145.3 20.8 %all-gather.3.cloned.1.call-done = bf16[2,64,8192]{2,1,0:T(8,128)(2,1)} async-done(((bf16[2,64,512]{2,1,0:T(8,128)(2,1)}), bf16[2,64,8192]{2,1,0:T(8,128)(2,1)}) %all-gather.3.cloned.1.call-update) | async-done | bytes 2097168 | tf_op jit(solution)/shard_map/all_gather | solution.py:110
  166.0 0.0 copy-start.1
  166.0 8.9 %fusion.3 = f32[2,64,1024]{2,1,0:T(8,128)S(1)} fusion(bf16[2,64,8192]{2,1,0:T(8,128)(2,1)} %all-gather.3.cloned.1.call-done, bf16[8192,1024]{1,0:T(8,128)(2,1)} %param.16), kind=kOutput, calls=%fused_computation.5 | convolution fusion | flops 2147483648 | bytes 19398656 | tf_op jit(solution)/shard_map/dot_general | solution.py:113
  174.9 0.0 copy-done.1
  174.9 8.3 %fusion.11 = bf16[2,64,1024]{2,1,0:T(8,128)(2,1)S(1)} fusion(bf16[2,64,8192]{2,1,0:T(8,128)(2,1)S(1)} %copy-done.1, bf16[8192,1024]{1,0:T(8,128)(2,1)} %param.17, f32[2,64,1024]{2,1,0:T(8,128)S(1)} %fusion.3), kind=kOutput, calls=%fused_computation.17 | convolution fusion | flops 2148270080 | bytes 19660800 | tf_op jit(solution)/shard_map/dot_general | solution.py:116
  183.3 1.1 gather_fusion.1
  184.4 0.7 broadcast_select_fusion
  (14 shorter events, 0.2 us)
Async XLA Ops:
  6.5 69.2 %copy-start = (bf16[1024,1024]{1,0:T(8,128)(2,1)S(1)}, bf16[1024,1024]{1,0:T(8,128)(2,1)}, u32[]{:S(2)}) copy-start(bf16[1024,1024]{1,0:T(8,128)(2,1)} %param.11) | copy-start | bytes 6291460
  44.9 4.9 %copy-start.3 = (bf16[2,16,8,16,64]{4,3,2,1,0:T(8,128)(2,1)S(1)}, bf16[2,16,8,16,64]{4,3,2,1,0:T(8,128)(2,1)}, u32[]{:S(2)}) copy-start(bf16[2,16,8,16,64]{4,3,2,1,0:T(8,128)(2,1)} %reshape.177) | copy-start | bytes 1572868
  52.2 8.4 %copy-start.2 = (bf16[2,1,128,1024]{3,2,1,0:T(8,128)(2,1)S(1)}, bf16[2,1,128,1024]{3,2,1,0:T(8,128)(2,1)}, u32[]{:S(2)}) copy-start(bf16[2,1,128,1024]{3,2,1,0:T(8,128)(2,1)} %param.9) | copy-start | bytes 1572868
  56.1 18.5 %all-to-all-start.1 = ((bf16[2,16,8,1024]{3,2,0,1:T(8,128)(2,1)}), bf16[2,16,8,1024]{3,2,0,1:T(8,128)(2,1)}, u32[]{:S(2)}, u32[]{:S(2)}) async-start(bf16[2,16,8,1024]{3,2,0,1:T(8,128)(2,1)} %reshape.202), calls=%async_computation.1 | async-start | bytes 1048576 | tf_op jit(solution)/shard_map/all_to_all | solution.py:73
  60.4 1.2 copy-start.5
  60.4 1.3 copy-start.6
  60.4 105.6 %all-gather.3.cloned.1.call-start = ((), (), s32[]{:S(2)}) async-start(), calls=%async_computation.2 | async-start | bytes 2228224 | tf_op jit(solution)/shard_map/all_gather | solution.py:110
  75.8 15.1 %copy-start.4 = (bf16[512]{0:T(512)(128)(2,1)S(1)}, bf16[512]{0:T(512)(128)(2,1)}, u32[]{:S(2)}) copy-start(bf16[512]{0:T(512)(128)(2,1)} %param.15) | copy-start | bytes 3076
  78.7 1.2 collective-permute-start
  80.0 4.0 %collective-permute-start.1 = (bf16[2,8,1024]{2,1,0:T(8,128)(2,1)S(1)}, bf16[2,8,1024]{2,1,0:T(8,128)(2,1)S(1)}, u32[]{:S(2)}, u32[]{:S(2)}) collective-permute-start(bf16[2,8,1024]{2,1,0:T(8,128)(2,1)S(1)} %maximum_select_fusion.4), channel_id=1, source_target_pairs={{0,2},{1,3},{2,0},{3,1},{4,6},{5,7},{6,4},{7,5},{8,10},{9,11},{10,... | collective-permute-start | bytes 98312 | tf_op jit(solution)/shard_map/ppermute | solution.py:89
  84.0 4.3 %collective-permute-start.2 = (bf16[2,16,1024]{2,1,0:T(8,128)(2,1)S(1)}, bf16[2,16,1024]{2,1,0:T(8,128)(2,1)S(1)}, u32[]{:S(2)}, u32[]{:S(2)}) collective-permute-start(bf16[2,16,1024]{2,1,0:T(8,128)(2,1)S(1)} %maximum_select_fusion.3), channel_id=1, source_target_pairs={{0,4},{1,5},{2,6},{3,7},{4,0},{5,1},{6,2},{7,3},{8,12},{9,13},{10,... | collective-permute-start | bytes 196616 | tf_op jit(solution)/shard_map/ppermute | solution.py:89
  88.3 7.3 %collective-permute-start.3 = (bf16[2,32,1024]{2,1,0:T(8,128)(2,1)S(1)}, bf16[2,32,1024]{2,1,0:T(8,128)(2,1)S(1)}, u32[]{:S(2)}, u32[]{:S(2)}) collective-permute-start(bf16[2,32,1024]{2,1,0:T(8,128)(2,1)S(1)} %maximum_select_fusion.2), channel_id=1, source_target_pairs={{0,8},{1,9},{2,10},{3,11},{4,12},{5,13},{6,14},{7,15},{8,0},{9,1},... | collective-permute-start | bytes 393224 | tf_op jit(solution)/shard_map/ppermute | solution.py:89
  166.0 8.9 %copy-start.1 = (bf16[2,64,8192]{2,1,0:T(8,128)(2,1)S(1)}, bf16[2,64,8192]{2,1,0:T(8,128)(2,1)}, u32[]{:S(2)}) copy-start(bf16[2,64,8192]{2,1,0:T(8,128)(2,1)} %all-gather.3.cloned.1.call-done) | copy-start | bytes 6291460
Sparse Core Ops, SparseCore 0:
  127.7 38.3 all-gather.2
